TPU v7x, 32 devices: a whole 2x2x4 slice. The times are simulated.
32 devices in a mesh: groups: 2 (over y), slide: 4 (over z), rep: 2 (over x), chan: 2 (over core).
Axes of the slice: x: 2, y: 2, z: 4, core: 2. Of those that a mesh axis runs over, the one named last changes fastest.
Arguments:
- tile_pixels: bfloat16 [4, 64, 6144], P(('groups', 'rep'), ('slide', 'chan')), parts along dimension 0, may hold values from -6 to 6
- tile_cell: int32 [4, 64], P(('groups', 'rep'), ('slide', 'chan')), parts along dimension 0, may hold values from -1 to 2047, as said below
- agg_cot: float32 [4, 64, 192, 128], P(('groups', 'rep'), 'slide', 'chan'), parts along dimension 0, may hold values from -6 to 6
- dw_weight: float32 [49, 96], replicated, may hold values from -0.6 to 0.6
- norm_gain: float32 [96], replicated, may hold values from 0.25 to 1.75
- up_weight: bfloat16 [96, 384], replicated, may hold values from -0.625 to 0.625
- proj_weight: bfloat16 [384, 96], replicated, may hold values from -0.3125 to 0.3125
- layer_scale: float32 [96], replicated, may hold values from 0.3 to 1
- ds_gain: float32 [96], replicated, may hold values from 0.25 to 1.75
- ds_weight: bfloat16 [384, 192], replicated, may hold values from -0.3125 to 0.3125
- agg_weight: bfloat16 [9, 192, 192], P(None, None, 'chan'), may hold values from -0.15625 to 0.15625
Outputs:
- agg_map: bfloat16 [4, 64, 192, 128], P(('groups', 'rep'), 'slide', 'chan'), parts along dimension 0
- agg_grad: float32 [18, 192, 192], P('groups', None, 'chan'), parts along dimension 0
- dw_grad: float32 [98, 96], P('groups'), parts along dimension 0
- up_grad: float32 [192, 384], P('groups'), parts along dimension 0
- proj_grad: float32 [768, 96], P('groups'), parts along dimension 0
- ds_grad: float32 [768, 192], P('groups'), parts along dimension 0
There are 2 independent parts, one for each index of `groups`. A program takes and returns all parts, laid end to end along the dimension named above; an argument that names none is the same for every part. Nothing has to cross between parts.
Inputs may be any that keep to these rules, and one draw needn't show every extreme that they name: `tile_cell`: A value r * 64 + q names a tile of grid row r and column q of a 32 x 64 slide grid; -1 marks an empty slot. No cell appears twice in one slide. Of the slots of one device (8 consecutive slots), at most 2 lie in one band of 8 tile rows, and in every slide one band holds exactly 2 tiles from every device.
All inputs are finite; a program needn't handle non-finite values.
Results may differ from a plain program's by a relative error of at most 0.018.
Values may be sent and summed in bfloat16 or wider, within the bound.
No kernel may reach another device: no remote copies, remote signals or barrier semaphores. Data moves between devices by JAX's collectives and lax.ppermute only.
A program may use at most 128 MiB of HBM per device.

v0:
```python
import math
import jax
import jax.numpy as jnp
from jax import lax
from jax.sharding import PartitionSpec as P

TILE_SIDE = 8
CAP = 2
GR = 8
GW = 64
BAND_CELLS = 512
FEAT = 3072


def shifted(value, axis, steps):
    count = lax.axis_size(axis)
    first, last = (max(0, -steps), min(count, count - steps))
    return lax.ppermute(value, axis, [(source, source + steps) for source in range(first, last)])


def layer_norm(values, gain):
    center = values - jnp.mean(values, axis=-1, keepdims=True)
    spread = jnp.mean(center * center, axis=-1, keepdims=True)
    return center * lax.rsqrt(spread + 1e-06) * gain


def stem(params, tile_rows):
    dw_weight, norm_gain, up_weight, proj_weight, layer_scale, ds_gain, ds_weight = params
    tile_count = tile_rows.shape[0]
    tile_side = TILE_SIDE
    channels = dw_weight.shape[1]
    inputs = tile_rows.reshape(tile_count, tile_side, tile_side, channels).astype(jnp.float32)
    padded = jnp.pad(inputs, ((0, 0), (3, 3), (3, 3), (0, 0)))
    spatial = jnp.zeros_like(inputs)
    for row_tap in range(7):
        for col_tap in range(7):
            spatial = (
                spatial
                + dw_weight[row_tap * 7 + col_tap]
                * padded[:, row_tap : row_tap + tile_side, col_tap : col_tap + tile_side, :]
            )
    normed = (
        layer_norm(spatial, norm_gain)
        .reshape(tile_count * tile_side * tile_side, channels)
        .astype(jnp.bfloat16)
    )
    hidden = jax.nn.gelu(
        jnp.dot(normed, up_weight, preferred_element_type=jnp.float32), approximate=False
    ).astype(jnp.bfloat16)
    branch = jnp.dot(hidden, proj_weight, preferred_element_type=jnp.float32)
    mixed_rows = inputs.reshape(tile_count * tile_side * tile_side, channels) + layer_scale * branch
    lowered = layer_norm(mixed_rows, ds_gain).astype(jnp.bfloat16)
    half_side = tile_side // 2
    patches = lowered.reshape(tile_count, half_side, 2, half_side, 2, channels).transpose(
        0, 1, 3, 2, 4, 5
    )
    patches = patches.reshape(tile_count * half_side * half_side, 4 * channels)
    result = jnp.dot(patches, ds_weight, preferred_element_type=jnp.float32)
    return result.reshape(tile_count, half_side * half_side * ds_weight.shape[1])


def aggregate(padded, weight_half):
    out_rows = (padded.shape[0] - 1) // 2
    out_cols = (padded.shape[1] - 1) // 2
    accumulated = jnp.zeros((out_rows * out_cols, weight_half.shape[2]), jnp.float32)
    for row_tap in range(3):
        for col_tap in range(3):
            window = padded[
                row_tap : row_tap + 2 * out_rows - 1 : 2,
                col_tap : col_tap + 2 * out_cols - 1 : 2,
                :,
            ]
            accumulated = accumulated + jnp.dot(
                window.reshape(out_rows * out_cols, padded.shape[2]),
                weight_half[row_tap * 3 + col_tap],
                preferred_element_type=jnp.float32,
            )
    return accumulated.reshape(out_rows, out_cols, weight_half.shape[2])


def on_device(
    tile_pixels,
    tile_cell,
    agg_cot,
    dw_weight,
    norm_gain,
    up_weight,
    proj_weight,
    layer_scale,
    ds_gain,
    ds_weight,
    agg_weight,
):
    params = (dw_weight, norm_gain, up_weight, proj_weight, layer_scale, ds_gain, ds_weight)
    tile_rows = tile_pixels[0]
    cell_ids = tile_cell[0]
    band_count = lax.axis_size("slide")
    chan_count = lax.axis_size("chan")
    feat_side = TILE_SIDE // 2
    checked_stem = jax.checkpoint(stem)
    tile_out, pull_stem = jax.vjp(lambda chosen: checked_stem(chosen, tile_rows), params)
    features = tile_out.astype(jnp.bfloat16)
    present = cell_ids >= 0
    dest_band = jnp.where(present, cell_ids // BAND_CELLS, band_count)
    within = jnp.where(present, cell_ids % BAND_CELLS, BAND_CELLS)
    slot_order = jnp.arange(cell_ids.shape[0], dtype=jnp.int32)
    earlier = (dest_band[:, None] == dest_band[None, :]) & (
        slot_order[None, :] < slot_order[:, None]
    )
    place_rank = jnp.sum(earlier.astype(jnp.int32), axis=1)
    position = jnp.where(present, dest_band * CAP + place_rank, band_count * CAP)
    send_rows = (
        jnp.zeros((band_count * CAP, FEAT), jnp.bfloat16).at[position].set(features, mode="drop")
    )
    send_cells = (
        jnp.full((band_count * CAP,), BAND_CELLS, jnp.int32).at[position].set(within, mode="drop")
    )
    own_rows, own_cells = (
        lax.all_to_all(send_rows, "slide", split_axis=0, concat_axis=0, tiled=True),
        lax.all_to_all(send_cells, "slide", split_axis=0, concat_axis=0, tiled=True),
    )
    recv_rows, recv_cells = (
        lax.all_gather(own_rows, "chan", axis=0, tiled=True),
        lax.all_gather(own_cells, "chan", axis=0, tiled=True),
    )
    cells_map = (
        jnp.zeros((BAND_CELLS, FEAT), jnp.bfloat16).at[recv_cells].set(recv_rows, mode="drop")
    )
    band_grid = cells_map.reshape(GR, GW, feat_side, feat_side, -1).transpose(0, 2, 1, 3, 4)
    band_grid = band_grid.reshape(GR * feat_side, GW * feat_side, -1)
    top_row = shifted(band_grid[-1], "slide", 1)
    padded = jnp.pad(jnp.concatenate([top_row[None], band_grid], axis=0), ((0, 0), (1, 0), (0, 0)))
    total_rows = agg_cot.shape[1] * band_count * lax.axis_size("rep") * agg_cot.shape[3]
    loss_scale = 1.0 / math.sqrt(total_rows)
    cotangent = agg_cot[0].transpose(0, 2, 1) * loss_scale
    result, pull_agg = jax.vjp(aggregate, padded, agg_weight)
    agg_map = result.astype(jnp.bfloat16).transpose(0, 2, 1)[None]
    d_padded, d_weight = pull_agg(cotangent)
    from_below = shifted(d_padded[0, 1:], "slide", -1)
    map_grad = (
        d_padded[1:, 1:]
        .astype(jnp.float32)
        .at[-1]
        .add(from_below.astype(jnp.float32))
        .astype(jnp.bfloat16)
    )
    grad_cells = (
        map_grad.reshape(GR, feat_side, GW, feat_side, -1)
        .transpose(0, 2, 1, 3, 4)
        .reshape(BAND_CELLS, FEAT)
    )
    slot_grads = jnp.where(
        (recv_cells < BAND_CELLS)[:, None],
        grad_cells[jnp.minimum(recv_cells, BAND_CELLS - 1)],
        jnp.zeros((), jnp.bfloat16),
    )
    by_source = slot_grads.reshape(chan_count, band_count, CAP, FEAT).transpose(1, 0, 2, 3)
    by_source = by_source.reshape(band_count * chan_count * CAP, FEAT)
    arrived = lax.all_to_all(by_source, "slide", split_axis=0, concat_axis=0, tiled=True)
    arrived = arrived.reshape(band_count, chan_count, CAP, FEAT).astype(jnp.float32)
    summed = lax.psum_scatter(
        arrived.astype(jnp.bfloat16), "chan", scatter_dimension=1, tiled=True
    ).astype(jnp.float32)
    gathered_grads = summed.reshape(band_count * CAP, FEAT)
    feature_grad = jnp.where(
        present[:, None], gathered_grads[jnp.minimum(position, band_count * CAP - 1)], 0.0
    )
    stem_grads = pull_stem(feature_grad)[0]
    dw_term = stem_grads[0]
    up_term = stem_grads[2].astype(jnp.float32)
    proj_term = stem_grads[3].astype(jnp.float32)
    ds_term = stem_grads[6].astype(jnp.float32)
    agg_term = d_weight.astype(jnp.float32)
    half_width = agg_term.shape[2]
    embedded = lax.dynamic_update_slice(
        jnp.zeros((9, agg_term.shape[1], half_width * chan_count), jnp.float32),
        agg_term,
        (0, 0, lax.axis_index("chan") * half_width),
    )
    summed_all = lax.psum(
        (dw_term, up_term, proj_term, ds_term, embedded), ("slide", "rep", "chan")
    )
    dw_grad = summed_all[0]
    up_grad = summed_all[1]
    proj_grad = summed_all[2]
    ds_grad = summed_all[3]
    agg_grad = lax.dynamic_slice_in_dim(
        summed_all[4], lax.axis_index("chan") * half_width, half_width, 2
    )
    return (agg_map, agg_grad, dw_grad, up_grad, proj_grad, ds_grad)


def solution(mesh):
    in_specs = (
        P(("groups", "rep"), ("slide", "chan"), None),
        P(("groups", "rep"), ("slide", "chan")),
        P(("groups", "rep"), "slide", "chan", None),
        P(),
        P(),
        P(),
        P(),
        P(),
        P(),
        P(),
        P(None, None, "chan"),
    )
    out_specs = (
        P(("groups", "rep"), "slide", "chan", None),
        P("groups", None, "chan"),
        P("groups", None),
        P("groups", None),
        P("groups", None),
        P("groups", None),
    )
    return jax.shard_map(
        on_device, mesh=mesh, in_specs=in_specs, out_specs=out_specs, check_vma=False
    )
```

profile of v0, /device:TPU:0, one launch (start us, length us, event | category | flops | bytes accessed | tf_op | source)
XLA Modules:
  0.0 863.3 jit_solution(13993026256152667323)
XLA Ops:
  18.9 31.2 %pad.226 = bf16[33,257,192]{1,2,0:T(8,128)(2,1)} pad(bf16[16,128,192]{1,2,0:T(8,128)(2,1)} %bitcast.629, bf16[]{:T(256)} %constant.57.clone.1), padding=2_0_1x2_0_1x0_0_0 | pad | bytes 4043138 | tf_op jit(solution)/shard_map/transpose(jvp())/pad | solution.py:68
  50.1 30.9 %pad.227 = bf16[33,257,192]{1,2,0:T(8,128)(2,1)} pad(bf16[16,128,192]{1,2,0:T(8,128)(2,1)} %bitcast.630, bf16[]{:T(256)} %constant.57.clone.1), padding=2_0_1x1_1_1x0_0_0 | pad | bytes 4043138 | tf_op jit(solution)/shard_map/transpose(jvp())/pad | solution.py:68
  83.2 31.0 %pad.228 = bf16[33,257,192]{1,2,0:T(8,128)(2,1)} pad(bf16[16,128,192]{1,2,0:T(8,128)(2,1)} %bitcast.631, bf16[]{:T(256)} %constant.57.clone.1), padding=2_0_1x0_2_1x0_0_0 | pad | bytes 4043138 | tf_op jit(solution)/shard_map/transpose(jvp())/pad | solution.py:68
  116.4 30.9 %pad.229 = bf16[33,257,192]{1,2,0:T(8,128)(2,1)} pad(bf16[16,128,192]{1,2,0:T(8,128)(2,1)} %bitcast.632, bf16[]{:T(256)} %constant.57.clone.1), padding=1_1_1x2_0_1x0_0_0 | pad | bytes 4043138 | tf_op jit(solution)/shard_map/transpose(jvp())/pad | solution.py:68
  149.5 30.9 %pad.230 = bf16[33,257,192]{1,2,0:T(8,128)(2,1)} pad(bf16[16,128,192]{1,2,0:T(8,128)(2,1)} %bitcast.633, bf16[]{:T(256)} %constant.57.clone.1), padding=1_1_1x1_1_1x0_0_0 | pad | bytes 4043138 | tf_op jit(solution)/shard_map/transpose(jvp())/pad | solution.py:68
  181.6 30.9 %pad.231 = bf16[33,257,192]{1,2,0:T(8,128)(2,1)} pad(bf16[16,128,192]{1,2,0:T(8,128)(2,1)} %bitcast.634, bf16[]{:T(256)} %constant.57.clone.1), padding=1_1_1x0_2_1x0_0_0 | pad | bytes 4043138 | tf_op jit(solution)/shard_map/transpose(jvp())/pad | solution.py:68
  212.6 30.6 %pad.232 = bf16[33,257,192]{1,2,0:T(8,128)(2,1)} pad(bf16[16,128,192]{1,2,0:T(8,128)(2,1)S(1)} %bitcast.635, bf16[]{:T(256)} %constant.57.clone.1), padding=0_2_1x2_0_1x0_0_0 | pad | bytes 4043138 | tf_op jit(solution)/shard_map/transpose(jvp())/pad | solution.py:68
  243.4 30.0 %pad.233 = bf16[33,257,192]{1,2,0:T(8,128)(2,1)} pad(bf16[16,128,192]{1,2,0:T(8,128)(2,1)S(1)} %bitcast.636, bf16[]{:T(256)} %constant.57.clone.1), padding=0_2_1x1_1_1x0_0_0 | pad | bytes 4043138 | tf_op jit(solution)/shard_map/transpose(jvp())/pad | solution.py:68
  273.6 30.0 %pad.234 = bf16[33,257,192]{1,2,0:T(8,128)(2,1)} pad(bf16[16,128,192]{1,2,0:T(8,128)(2,1)S(1)} %bitcast.637, bf16[]{:T(256)} %constant.57.clone.1), padding=0_2_1x0_2_1x0_0_0 | pad | bytes 4043138 | tf_op jit(solution)/shard_map/transpose(jvp())/pad | solution.py:68
  303.6 14.5 %add_add_fusion = bf16[33,257,192]{1,2,0:T(8,128)(2,1)S(1)} fusion(bf16[33,257,192]{1,2,0:T(8,128)(2,1)} %pad.234, bf16[33,257,192]{1,2,0:T(8,128)(2,1)} %pad.233, bf16[33,257,192]{1,2,0:T(8,128)(2,1)} %pad.232, bf16[33,257,192]{1,2,0:T(8,128)(2,1)} %pad.231, bf16[33,257,192]{1,2,0:T(8,128)(2,1)} %pad.230, bf16[33,257,192]{1,2,0:T(8,128)(2,1)} %pad.229, ...), kind=kLoop, calls=%fused_computation.105 | loop fusion | flops 13026816 | bytes 32567040 | tf_op jit(solution)/shard_map/transpose(jvp())/add_any | solution.py:68
  323.3 8.2 all-to-all-start
  417.1 8.5 reshape.737
  440.5 28.5 %slice.767 = bf16[16,128,192]{1,2,0:T(8,128)(2,1)S(1)} slice(bf16[33,257,192]{1,2,0:T(8,128)(2,1)} %fusion.2), slice={[0:31:2], [0:255:2], [0:192:1]} | slice | bytes 1572864 | tf_op jit(solution)/shard_map/jvp()/slice | solution.py:68
  469.1 28.7 %slice.769 = bf16[16,128,192]{1,2,0:T(8,128)(2,1)} slice(bf16[33,257,192]{1,2,0:T(8,128)(2,1)} %fusion.2), slice={[0:31:2], [1:256:2], [0:192:1]} | slice | bytes 1572864 | tf_op jit(solution)/shard_map/jvp()/slice | solution.py:68
  497.8 28.7 %slice.771 = bf16[16,128,192]{1,2,0:T(8,128)(2,1)} slice(bf16[33,257,192]{1,2,0:T(8,128)(2,1)} %fusion.2), slice={[0:31:2], [2:257:2], [0:192:1]} | slice | bytes 1572864 | tf_op jit(solution)/shard_map/jvp()/slice | solution.py:68
  526.5 28.8 %slice.773 = bf16[16,128,192]{1,2,0:T(8,128)(2,1)} slice(bf16[33,257,192]{1,2,0:T(8,128)(2,1)} %fusion.2), slice={[1:32:2], [0:255:2], [0:192:1]} | slice | bytes 1572864 | tf_op jit(solution)/shard_map/jvp()/slice | solution.py:68
  555.3 28.7 %slice.775 = bf16[16,128,192]{1,2,0:T(8,128)(2,1)} slice(bf16[33,257,192]{1,2,0:T(8,128)(2,1)} %fusion.2), slice={[1:32:2], [1:256:2], [0:192:1]} | slice | bytes 1572864 | tf_op jit(solution)/shard_map/jvp()/slice | solution.py:68
  584.0 28.7 %slice.777 = bf16[16,128,192]{1,2,0:T(8,128)(2,1)} slice(bf16[33,257,192]{1,2,0:T(8,128)(2,1)} %fusion.2), slice={[1:32:2], [2:257:2], [0:192:1]} | slice | bytes 1572864 | tf_op jit(solution)/shard_map/jvp()/slice | solution.py:68
  612.7 28.9 %slice.779 = bf16[16,128,192]{1,2,0:T(8,128)(2,1)} slice(bf16[33,257,192]{1,2,0:T(8,128)(2,1)} %fusion.2), slice={[2:33:2], [0:255:2], [0:192:1]} | slice | bytes 1572864 | tf_op jit(solution)/shard_map/jvp()/slice | solution.py:68
  641.7 28.2 %slice.781 = bf16[16,128,192]{1,2,0:T(8,128)(2,1)S(1)} slice(bf16[33,257,192]{1,2,0:T(8,128)(2,1)} %fusion.2), slice={[2:33:2], [1:256:2], [0:192:1]} | slice | bytes 1572864 | tf_op jit(solution)/shard_map/jvp()/slice | solution.py:68
  669.9 28.3 %slice.783 = bf16[16,128,192]{1,2,0:T(8,128)(2,1)S(1)} slice(bf16[33,257,192]{1,2,0:T(8,128)(2,1)} %fusion.2), slice={[2:33:2], [2:257:2], [0:192:1]} | slice | bytes 1572864 | tf_op jit(solution)/shard_map/jvp()/slice | solution.py:68
  716.1 15.7 %all-reduce.76.cloned.1.call-done = bf16[4,2,2,3072]{3,0,2,1:T(4,128)(2,1)} async-done(((bf16[4,2,2,3072]{3,0,2,1:T(4,128)(2,1)}), bf16[4,2,2,3072]{3,0,2,1:T(4,128)(2,1)}) %all-reduce.76.cloned.1.call-update) | async-done | bytes 98320
  750.0 62.6 %psum.36 = f32[49,96]{1,0:T(8,128)} all-reduce(f32[49,96]{1,0:T(8,128)S(1)} %pad_add_fusion), channel_id=1, replica_groups=mesh['groups'=2,'slide'=4,'rep'=2,'chan'=2] {'slide','rep','chan'}, use_global_device_ids=true, to_apply=%region_67.68 | all-reduce | flops 4704 | bytes 37632 | tf_op jit(solution)/shard_map/psum | solution.py:180
  812.6 36.1 %all-reduce.78.cloned.1.call-done = (f32[9,192,192]{2,1,0:T(8,128)}, f32[96,384]{1,0:T(8,128)}, f32[384,96]{0,1:T(8,128)}, f32[384,192]{0,1:T(8,128)}) async-done(((f32[9,192,192]{2,1,0:T(8,128)}, f32[96,384]{1,0:T(8,128)}, f32[384,96]{0,1:T(8,128)}, f32[384,192]{0,1:T(8,128)}), (f32[9,192,192]{2,1,0:T(8,128)}, f32[96,384]{1,0:T(8,128)}, f32[384,96]{0,1:T(8,128)}, ...) | async-done | bytes 1916944 | tf_op jit(solution)/shard_map/psum | solution.py:180
  (234 shorter events, 167.8 us)
Async XLA Ops:
  7.2 336.5 %copy-start = (bf16[384,192]{0,1:T(8,128)(2,1)S(1)}, bf16[384,192]{0,1:T(8,128)(2,1)}, u32[]{:S(2)}) copy-start(bf16[384,192]{0,1:T(8,128)(2,1)} %param.22) | copy-start | bytes 442372
  303.6 18.2 %copy-start.31 = (s32[1,8]{1,0:T(1,128)S(1)}, s32[1,8]{1,0:T(1,128)}, u32[]{:S(2)}) copy-start(s32[1,8]{1,0:T(1,128)} %param.14) | copy-start | bytes 100
  320.4 18.1 %copy-start.20 = (f32[49,96]{1,0:T(8,128)S(1)}, f32[49,96]{1,0:T(8,128)}, u32[]{:S(2)}) copy-start(f32[49,96]{1,0:T(8,128)} %param.16) | copy-start | bytes 56452
  320.4 18.1 %copy-start.12 = (bf16[1,8,6144]{2,1,0:T(8,128)(2,1)S(1)}, bf16[1,8,6144]{2,1,0:T(8,128)(2,1)}, u32[]{:S(2)}) copy-start(bf16[1,8,6144]{2,1,0:T(8,128)(2,1)} %param.13) | copy-start | bytes 294916
  320.5 71.1 %collective-permute-start.1 = (bf16[256,192]{0,1:T(8,128)(2,1)S(1)}, bf16[256,192]{0,1:T(8,128)(2,1)}, u32[]{:S(2)}, u32[]{:S(2)}) collective-permute-start(bf16[256,192]{0,1:T(8,128)(2,1)S(1)} %slice_bitcast_fusion), channel_id=1, source_target_pairs={{4,0},{8,4},{12,8},{5,1},{9,5},{13,9},{6,2},{10,6},{14,10},{7,3},{... | collective-permute-start | bytes 294920 | tf_op jit(solution)/shard_map/ppermute | solution.py:18
  323.3 23.4 %all-to-all-start = ((s32[4,2,1]{1,2,0:T(1,128)}), s32[4,2,1]{1,2,0:T(1,128)S(1)}, u32[]{:S(2)}, u32[]{:S(2)}) async-start(s32[4,2,1]{1,2,0:T(1,128)} %bitcast.5), calls=%async_computation | async-start | bytes 4096 | tf_op jit(solution)/shard_map/all_to_all | solution.py:120
  331.5 9.3 %copy-start.26 = (f32[96]{0:T(128)S(1)}, f32[96]{0:T(128)}, u32[]{:S(2)}) copy-start(f32[96]{0:T(128)} %param.17) | copy-start | bytes 1156
  331.5 9.5 %copy-start.22 = (bf16[384,96]{0,1:T(8,128)(2,1)S(1)}, bf16[384,96]{0,1:T(8,128)(2,1)}, u32[]{:S(2)}) copy-start(bf16[384,96]{0,1:T(8,128)(2,1)} %param.19) | copy-start | bytes 221188
  331.5 9.5 %copy-start.24 = (bf16[96,384]{1,0:T(8,128)(2,1)S(1)}, bf16[96,384]{1,0:T(8,128)(2,1)}, u32[]{:S(2)}) copy-start(bf16[96,384]{1,0:T(8,128)(2,1)} %param.18) | copy-start | bytes 221188
  331.5 9.5 %copy-start.28 = (f32[96]{0:T(128)S(1)}, f32[96]{0:T(128)}, u32[]{:S(2)}) copy-start(f32[96]{0:T(128)} %param.20) | copy-start | bytes 1156
  346.7 10.8 %all-to-all-start.1 = ((bf16[4,2,3072]{2,1,0:T(2,128)(2,1)}), bf16[4,2,3072]{2,1,0:T(2,128)(2,1)S(1)}, u32[]{:S(2)}, u32[]{:S(2)}) async-start(bf16[4,2,3072]{2,1,0:T(2,128)(2,1)} %all_to_all.25), calls=%async_computation.1 | async-start | bytes 98304 | tf_op jit(solution)/shard_map/all_to_all | solution.py:119
  388.2 46.2 %collective-permute-start = (bf16[256,192]{0,1:T(8,128)(2,1)}, bf16[256,192]{0,1:T(8,128)(2,1)}, u32[]{:S(2)}, u32[]{:S(2)}) collective-permute-start(bf16[256,192]{0,1:T(8,128)(2,1)} %slice_bitcast_fusion.1), channel_id=1, source_target_pairs={{0,4},{4,8},{8,12},{1,5},{5,9},{9,13},{2,6},{6,10},{10,14},{3,7},{... | collective-permute-start | bytes 294920 | tf_op jit(solution)/shard_map/ppermute | solution.py:18
  431.0 280.7 %all-to-all-start.2 = ((bf16[4,4,3072]{2,1,0:T(4,128)(2,1)}), bf16[4,4,3072]{2,1,0:T(4,128)(2,1)S(1)}, u32[]{:S(2)}, u32[]{:S(2)}) async-start(bf16[4,4,3072]{2,1,0:T(4,128)(2,1)} %copy.135), calls=%async_computation.2 | async-start | bytes 196608 | tf_op jit(solution)/shard_map/all_to_all | solution.py:159
  434.3 297.5 %all-reduce.76.cloned.1.call-start = ((), (), s32[]{:S(2)}) async-start(), calls=%async_computation.3 | async-start | bytes 196608
  526.5 171.7 %copy-start.1 = (f32[1,16,96,128]{3,2,1,0:T(8,128)S(1)}, f32[1,16,96,128]{3,2,1,0:T(8,128)}, u32[]{:S(2)}) copy-start(f32[1,16,96,128]{3,2,1,0:T(8,128)} %param.15) | copy-start | bytes 2359300
  698.2 5.8 copy-start.5
  698.2 6.8 copy-start.4
  698.6 7.4 copy-start.3
  702.0 5.9 copy-start.8
  702.0 5.9 copy-start.11
  710.2 23.7 %copy-start.30 = (pred[8]{0:T(512)(128)(4,1)S(1)}, pred[8]{0:T(512)(128)(4,1)}, u32[]{:S(2)}) copy-start(pred[8]{0:T(512)(128)(4,1)} %bitcast_compare_fusion) | copy-start | bytes 28
  710.2 23.8 %copy-start.21 = (f32[49,96]{1,0:T(8,128)S(1)}, f32[49,96]{1,0:T(8,128)}, u32[]{:S(2)}) copy-start(f32[49,96]{1,0:T(8,128)} %param.16) | copy-start | bytes 56452
  712.5 136.2 %all-reduce.78.cloned.1.call-start = ((), (), s32[]{:S(2)}) async-start(), calls=%async_computation.4 | async-start | bytes 4718592 | tf_op jit(solution)/shard_map/psum | solution.py:180
  716.1 24.3 %copy-start.9 = (f32[9,192,192]{2,1,0:T(8,128)}, f32[9,192,192]{2,1,0:T(8,128)S(1)}, u32[]{:S(2)}) copy-start(f32[9,192,192]{2,1,0:T(8,128)S(1)} %dynamic_update_slice.3) | copy-start | bytes 3981316
  (15 other events, 52.3 us)
Sparse Core Ops, SparseCore 0:
  712.6 19.1 all-reduce.75
  748.1 100.5 all-reduce.77
where the time goes:
time: 869 us; the launch traced here: 863 us
  local copies, waits for them, and re-layouts  629 us (72%)
  blocking collectives  66.4 us (8%)
  waiting for transfers between devices  54.1 us (6%)
  other arithmetic  44.9 us (5%)
  matrix products  32.1 us (4%)
  starting transfers between devices  21.3 us (2%)
  between operations  16 us (2%)
    pad x9, local copies, waits for them, and re-layouts, aggregate(): padded[row_tap:row_tap + 2 * out_rows - 1:2, col_tap:col_tap + 2 * out_co...  276 us
    slice x9, local copies, waits for them, and re-layouts, aggregate(): padded[row_tap:row_tap + 2 * out_rows - 1:2, col_tap:col_tap + 2 * out_co...  258 us
    psum x1, blocking collectives, on_device(): lax.psum((dw_term, up_term, proj_term, ds_term, embedded), ('slide', 'rep...  62.6 us
    psum x1, waiting for transfers between devices, on_device(): lax.psum((dw_term, up_term, proj_term, ds_term, embedded), ('slide', 'rep...  36.1 us
    dot_general x27, matrix products, aggregate(): jnp.dot(window.reshape(out_rows * out_cols, padded.shape[2]), weight_half...  20.7 us
  transfers between devices with their start and end apart: 7, of which 3 were waited for; matrix products, arithmetic and copies ran while one was open for 42% of the time, Pallas kernels for 0%

commit v1 on v0

--- a/solution.py
+++ b/solution.py
@@ -178,7 +178,7 @@
         (0, 0, lax.axis_index("chan") * half_width),
     )
     summed_all = lax.psum(
-        (dw_term, up_term, proj_term, ds_term, embedded), ("slide", "rep", "chan")
+        lax.psum((dw_term, up_term, proj_term, ds_term, embedded), ("rep", "chan")), "slide"
     )
     dw_grad = summed_all[0]
     up_grad = summed_all[1]

time: 869 us -> 933 us (1.074)
  waiting for transfers between devices: 54.1 us -> 131 us
  blocking collectives: 66.4 us -> 36.1 us
  matrix products: 32.1 us -> 42.2 us
    psum x1 -> x2, waiting for transfers between devices: 36.1 us -> 116 us  [the longest x1 64.9 us: on_device(): lax.psum(lax.psum((dw_term, up_term, proj_term, ds_term, embedded), ('rep...]
    psum x1 -> x2, blocking collectives: 62.6 us -> 32.3 us  [the longest x1 21.6 us: on_device(): lax.psum(lax.psum((dw_term, up_term, proj_term, ds_term, embedded), ('rep...]
  transfers between devices with their start and end apart: 7 -> 8, of which waited for: 3 -> 4; matrix products, arithmetic and copies ran while one was open for 42% -> 41% of each run, Pallas kernels for 0% -> 0%
where the time goes in v1:
time: 933 us; the launch traced here: 927 us
  local copies, waits for them, and re-layouts  634 us (68%)
  waiting for transfers between devices  131 us (14%)
  other arithmetic  46.2 us (5%)
  matrix products  42.2 us (5%)
  blocking collectives  36.1 us (4%)
  starting transfers between devices  21.3 us (2%)
  between operations  15.8 us (2%)
    pad x9, local copies, waits for them, and re-layouts, aggregate(): padded[row_tap:row_tap + 2 * out_rows - 1:2, col_tap:col_tap + 2 * out_co...  276 us
    slice x9, local copies, waits for them, and re-layouts, aggregate(): padded[row_tap:row_tap + 2 * out_rows - 1:2, col_tap:col_tap + 2 * out_co...  258 us
    psum x1, waiting for transfers between devices, on_device(): lax.psum(lax.psum((dw_term, up_term, proj_term, ds_term, embedded), ('rep...  64.9 us
    psum x1, waiting for transfers between devices, on_device(): lax.psum((dw_term, up_term, proj_term, ds_term, embedded), ('rep', 'chan'))  51.5 us
    dot_general x27, matrix products, aggregate(): jnp.dot(window.reshape(out_rows * out_cols, padded.shape[2]), weight_half...  28.8 us
    psum x1, blocking collectives, on_device(): lax.psum(lax.psum((dw_term, up_term, proj_term, ds_term, embedded), ('rep...  21.6 us
  transfers between devices with their start and end apart: 8, of which 4 were waited for; matrix products, arithmetic and copies ran while one was open for 41% of the time, Pallas kernels for 0%

profile of v1, /device:TPU:0, one launch (start us, length us, event | category | flops | bytes accessed | tf_op | source)
XLA Modules:
  0.0 927.1 jit_solution(11889875329132915643)
XLA Ops:
  18.9 31.2 %pad.226 = bf16[33,257,192]{1,2,0:T(8,128)(2,1)} pad(bf16[16,128,192]{1,2,0:T(8,128)(2,1)} %bitcast.629, bf16[]{:T(256)} %constant.57.clone.1), padding=2_0_1x2_0_1x0_0_0 | pad | bytes 4043138 | tf_op jit(solution)/shard_map/transpose(jvp())/pad | solution.py:68
  50.1 30.9 %pad.227 = bf16[33,257,192]{1,2,0:T(8,128)(2,1)} pad(bf16[16,128,192]{1,2,0:T(8,128)(2,1)} %bitcast.630, bf16[]{:T(256)} %constant.57.clone.1), padding=2_0_1x1_1_1x0_0_0 | pad | bytes 4043138 | tf_op jit(solution)/shard_map/transpose(jvp())/pad | solution.py:68
  83.2 31.0 %pad.228 = bf16[33,257,192]{1,2,0:T(8,128)(2,1)} pad(bf16[16,128,192]{1,2,0:T(8,128)(2,1)} %bitcast.631, bf16[]{:T(256)} %constant.57.clone.1), padding=2_0_1x0_2_1x0_0_0 | pad | bytes 4043138 | tf_op jit(solution)/shard_map/transpose(jvp())/pad | solution.py:68
  116.4 30.9 %pad.229 = bf16[33,257,192]{1,2,0:T(8,128)(2,1)} pad(bf16[16,128,192]{1,2,0:T(8,128)(2,1)} %bitcast.632, bf16[]{:T(256)} %constant.57.clone.1), padding=1_1_1x2_0_1x0_0_0 | pad | bytes 4043138 | tf_op jit(solution)/shard_map/transpose(jvp())/pad | solution.py:68
  149.5 30.9 %pad.230 = bf16[33,257,192]{1,2,0:T(8,128)(2,1)} pad(bf16[16,128,192]{1,2,0:T(8,128)(2,1)} %bitcast.633, bf16[]{:T(256)} %constant.57.clone.1), padding=1_1_1x1_1_1x0_0_0 | pad | bytes 4043138 | tf_op jit(solution)/shard_map/transpose(jvp())/pad | solution.py:68
  181.6 30.9 %pad.231 = bf16[33,257,192]{1,2,0:T(8,128)(2,1)} pad(bf16[16,128,192]{1,2,0:T(8,128)(2,1)} %bitcast.634, bf16[]{:T(256)} %constant.57.clone.1), padding=1_1_1x0_2_1x0_0_0 | pad | bytes 4043138 | tf_op jit(solution)/shard_map/transpose(jvp())/pad | solution.py:68
  212.6 30.6 %pad.232 = bf16[33,257,192]{1,2,0:T(8,128)(2,1)} pad(bf16[16,128,192]{1,2,0:T(8,128)(2,1)S(1)} %bitcast.635, bf16[]{:T(256)} %constant.57.clone.1), padding=0_2_1x2_0_1x0_0_0 | pad | bytes 4043138 | tf_op jit(solution)/shard_map/transpose(jvp())/pad | solution.py:68
  243.4 30.0 %pad.233 = bf16[33,257,192]{1,2,0:T(8,128)(2,1)} pad(bf16[16,128,192]{1,2,0:T(8,128)(2,1)S(1)} %bitcast.636, bf16[]{:T(256)} %constant.57.clone.1), padding=0_2_1x1_1_1x0_0_0 | pad | bytes 4043138 | tf_op jit(solution)/shard_map/transpose(jvp())/pad | solution.py:68
  273.6 30.0 %pad.234 = bf16[33,257,192]{1,2,0:T(8,128)(2,1)} pad(bf16[16,128,192]{1,2,0:T(8,128)(2,1)S(1)} %bitcast.637, bf16[]{:T(256)} %constant.57.clone.1), padding=0_2_1x0_2_1x0_0_0 | pad | bytes 4043138 | tf_op jit(solution)/shard_map/transpose(jvp())/pad | solution.py:68
  303.6 14.5 %add_add_fusion = bf16[33,257,192]{1,2,0:T(8,128)(2,1)S(1)} fusion(bf16[33,257,192]{1,2,0:T(8,128)(2,1)} %pad.234, bf16[33,257,192]{1,2,0:T(8,128)(2,1)} %pad.233, bf16[33,257,192]{1,2,0:T(8,128)(2,1)} %pad.232, bf16[33,257,192]{1,2,0:T(8,128)(2,1)} %pad.231, bf16[33,257,192]{1,2,0:T(8,128)(2,1)} %pad.230, bf16[33,257,192]{1,2,0:T(8,128)(2,1)} %pad.229, ...), kind=kLoop, calls=%fused_computation.105 | loop fusion | flops 13026816 | bytes 32567040 | tf_op jit(solution)/shard_map/transpose(jvp())/add_any | solution.py:68
  440.0 28.5 %slice.767 = bf16[16,128,192]{1,2,0:T(8,128)(2,1)S(1)} slice(bf16[33,257,192]{1,2,0:T(8,128)(2,1)} %fusion.2), slice={[0:31:2], [0:255:2], [0:192:1]} | slice | bytes 1572864 | tf_op jit(solution)/shard_map/jvp()/slice | solution.py:68
  468.5 28.7 %slice.769 = bf16[16,128,192]{1,2,0:T(8,128)(2,1)} slice(bf16[33,257,192]{1,2,0:T(8,128)(2,1)} %fusion.2), slice={[0:31:2], [1:256:2], [0:192:1]} | slice | bytes 1572864 | tf_op jit(solution)/shard_map/jvp()/slice | solution.py:68
  497.2 28.7 %slice.771 = bf16[16,128,192]{1,2,0:T(8,128)(2,1)} slice(bf16[33,257,192]{1,2,0:T(8,128)(2,1)} %fusion.2), slice={[0:31:2], [2:257:2], [0:192:1]} | slice | bytes 1572864 | tf_op jit(solution)/shard_map/jvp()/slice | solution.py:68
  525.9 28.8 %slice.773 = bf16[16,128,192]{1,2,0:T(8,128)(2,1)} slice(bf16[33,257,192]{1,2,0:T(8,128)(2,1)} %fusion.2), slice={[1:32:2], [0:255:2], [0:192:1]} | slice | bytes 1572864 | tf_op jit(solution)/shard_map/jvp()/slice | solution.py:68
  554.7 28.7 %slice.775 = bf16[16,128,192]{1,2,0:T(8,128)(2,1)} slice(bf16[33,257,192]{1,2,0:T(8,128)(2,1)} %fusion.2), slice={[1:32:2], [1:256:2], [0:192:1]} | slice | bytes 1572864 | tf_op jit(solution)/shard_map/jvp()/slice | solution.py:68
  583.4 28.8 %slice.777 = bf16[16,128,192]{1,2,0:T(8,128)(2,1)} slice(bf16[33,257,192]{1,2,0:T(8,128)(2,1)} %fusion.2), slice={[1:32:2], [2:257:2], [0:192:1]} | slice | bytes 1572864 | tf_op jit(solution)/shard_map/jvp()/slice | solution.py:68
  612.2 28.9 %slice.779 = bf16[16,128,192]{1,2,0:T(8,128)(2,1)} slice(bf16[33,257,192]{1,2,0:T(8,128)(2,1)} %fusion.2), slice={[2:33:2], [0:255:2], [0:192:1]} | slice | bytes 1572864 | tf_op jit(solution)/shard_map/jvp()/slice | solution.py:68
  641.1 28.2 %slice.781 = bf16[16,128,192]{1,2,0:T(8,128)(2,1)S(1)} slice(bf16[33,257,192]{1,2,0:T(8,128)(2,1)} %fusion.2), slice={[2:33:2], [1:256:2], [0:192:1]} | slice | bytes 1572864 | tf_op jit(solution)/shard_map/jvp()/slice | solution.py:68
  669.3 28.3 %slice.783 = bf16[16,128,192]{1,2,0:T(8,128)(2,1)S(1)} slice(bf16[33,257,192]{1,2,0:T(8,128)(2,1)} %fusion.2), slice={[2:33:2], [2:257:2], [0:192:1]} | slice | bytes 1572864 | tf_op jit(solution)/shard_map/jvp()/slice | solution.py:68
  720.6 12.7 %all-reduce.78.cloned.1.call-done = bf16[4,2,2,3072]{3,0,2,1:T(4,128)(2,1)} async-done(((bf16[4,2,2,3072]{3,0,2,1:T(4,128)(2,1)}), bf16[4,2,2,3072]{3,0,2,1:T(4,128)(2,1)}) %all-reduce.78.cloned.1.call-update) | async-done | bytes 98320
  761.0 51.5 %all-reduce.80.cloned.1.call-done = (f32[9,192,192]{2,1,0:T(8,128)}, f32[96,384]{1,0:T(8,128)}, f32[384,96]{0,1:T(8,128)}, f32[384,192]{0,1:T(8,128)}) async-done(((f32[9,192,192]{2,1,0:T(8,128)}, f32[96,384]{1,0:T(8,128)}, f32[384,96]{0,1:T(8,128)}, f32[384,192]{0,1:T(8,128)}), (f32[9,192,192]{2,1,0:T(8,128)}, f32[96,384]{1,0:T(8,128)}, f32[384,96]{0,1:T(8,128)}, ...) | async-done | bytes 1916944 | tf_op jit(solution)/shard_map/psum | solution.py:181
  815.6 10.7 %psum.72 = f32[49,96]{1,0:T(8,128)S(1)} all-reduce(f32[49,96]{1,0:T(8,128)S(1)} %pad_add_fusion), channel_id=1, replica_groups=mesh['groups'=2,'slide'=4,'rep'=2,'chan'=2] {'rep','chan'}, use_global_device_ids=true, to_apply=%region_68.69 | all-reduce | flops 4704 | bytes 37632 | tf_op jit(solution)/shard_map/psum | solution.py:181
  826.3 21.6 %psum.73 = f32[49,96]{1,0:T(8,128)} all-reduce(f32[49,96]{1,0:T(8,128)S(1)} %psum.72), channel_id=1, replica_groups=mesh['groups'=2,'slide'=4,'rep'=2,'chan'=2] {'slide'}, use_global_device_ids=true, to_apply=%region_69.70 | all-reduce | flops 4704 | bytes 37632 | tf_op jit(solution)/shard_map/psum | solution.py:180
  847.9 64.9 %all-reduce.82.cloned.1.call-done = (f32[9,192,192]{2,1,0:T(8,128)}, f32[96,384]{1,0:T(8,128)}, f32[384,96]{0,1:T(8,128)}, f32[384,192]{0,1:T(8,128)}) async-done(((f32[9,192,192]{2,1,0:T(8,128)}, f32[96,384]{1,0:T(8,128)}, f32[384,96]{0,1:T(8,128)}, f32[384,192]{0,1:T(8,128)}), (f32[9,192,192]{2,1,0:T(8,128)}, f32[96,384]{1,0:T(8,128)}, f32[384,96]{0,1:T(8,128)}, ...) | async-done | bytes 1916944 | tf_op jit(solution)/shard_map/psum | solution.py:180
  (252 shorter events, 201.5 us)
Async XLA Ops:
  7.2 335.9 %copy-start = (bf16[384,192]{0,1:T(8,128)(2,1)S(1)}, bf16[384,192]{0,1:T(8,128)(2,1)}, u32[]{:S(2)}) copy-start(bf16[384,192]{0,1:T(8,128)(2,1)} %param.22) | copy-start | bytes 442372
  303.6 18.2 %copy-start.38 = (s32[1,8]{1,0:T(1,128)S(1)}, s32[1,8]{1,0:T(1,128)}, u32[]{:S(2)}) copy-start(s32[1,8]{1,0:T(1,128)} %param.14) | copy-start | bytes 100
  320.4 17.5 %copy-start.27 = (f32[49,96]{1,0:T(8,128)S(1)}, f32[49,96]{1,0:T(8,128)}, u32[]{:S(2)}) copy-start(f32[49,96]{1,0:T(8,128)} %param.16) | copy-start | bytes 56452
  320.4 17.5 %copy-start.14 = (bf16[1,8,6144]{2,1,0:T(8,128)(2,1)S(1)}, bf16[1,8,6144]{2,1,0:T(8,128)(2,1)}, u32[]{:S(2)}) copy-start(bf16[1,8,6144]{2,1,0:T(8,128)(2,1)} %param.13) | copy-start | bytes 294916
  320.5 70.5 %collective-permute-start.1 = (bf16[256,192]{0,1:T(8,128)(2,1)S(1)}, bf16[256,192]{0,1:T(8,128)(2,1)}, u32[]{:S(2)}, u32[]{:S(2)}) collective-permute-start(bf16[256,192]{0,1:T(8,128)(2,1)S(1)} %slice_bitcast_fusion), channel_id=1, source_target_pairs={{4,0},{8,4},{12,8},{5,1},{9,5},{13,9},{6,2},{10,6},{14,10},{7,3},{... | collective-permute-start | bytes 294920 | tf_op jit(solution)/shard_map/ppermute | solution.py:18
  323.3 22.9 %all-to-all-start = ((s32[4,2,1]{1,2,0:T(1,128)}), s32[4,2,1]{1,2,0:T(1,128)S(1)}, u32[]{:S(2)}, u32[]{:S(2)}) async-start(s32[4,2,1]{1,2,0:T(1,128)} %bitcast.5), calls=%async_computation | async-start | bytes 4096 | tf_op jit(solution)/shard_map/all_to_all | solution.py:120
  331.5 8.8 copy-start.33
  331.5 9.0 copy-start.29
  331.5 9.0 copy-start.31
  331.5 9.0 copy-start.36
  346.2 10.8 %all-to-all-start.1 = ((bf16[4,2,3072]{2,1,0:T(2,128)(2,1)}), bf16[4,2,3072]{2,1,0:T(2,128)(2,1)S(1)}, u32[]{:S(2)}, u32[]{:S(2)}) async-start(bf16[4,2,3072]{2,1,0:T(2,128)(2,1)} %all_to_all.25), calls=%async_computation.1 | async-start | bytes 98304 | tf_op jit(solution)/shard_map/all_to_all | solution.py:119
  387.6 46.2 %collective-permute-start = (bf16[256,192]{0,1:T(8,128)(2,1)}, bf16[256,192]{0,1:T(8,128)(2,1)}, u32[]{:S(2)}, u32[]{:S(2)}) collective-permute-start(bf16[256,192]{0,1:T(8,128)(2,1)} %slice_bitcast_fusion.1), channel_id=1, source_target_pairs={{0,4},{4,8},{8,12},{1,5},{5,9},{9,13},{2,6},{6,10},{10,14},{3,7},{... | collective-permute-start | bytes 294920 | tf_op jit(solution)/shard_map/ppermute | solution.py:18
  430.4 282.8 %all-to-all-start.2 = ((bf16[4,4,3072]{2,1,0:T(4,128)(2,1)}), bf16[4,4,3072]{2,1,0:T(4,128)(2,1)S(1)}, u32[]{:S(2)}, u32[]{:S(2)}) async-start(bf16[4,4,3072]{2,1,0:T(4,128)(2,1)} %copy.135), calls=%async_computation.2 | async-start | bytes 196608 | tf_op jit(solution)/shard_map/all_to_all | solution.py:159
  433.7 299.6 %all-reduce.78.cloned.1.call-start = ((), (), s32[]{:S(2)}) async-start(), calls=%async_computation.3 | async-start | bytes 196608
  525.9 171.7 %copy-start.1 = (f32[1,16,96,128]{3,2,1,0:T(8,128)S(1)}, f32[1,16,96,128]{3,2,1,0:T(8,128)}, u32[]{:S(2)}) copy-start(f32[1,16,96,128]{3,2,1,0:T(8,128)} %param.15) | copy-start | bytes 2359300
  698.0 7.4 copy-start.3
  710.9 24.7 %copy-start.28 = (f32[49,96]{1,0:T(8,128)S(1)}, f32[49,96]{1,0:T(8,128)}, u32[]{:S(2)}) copy-start(f32[49,96]{1,0:T(8,128)} %param.16) | copy-start | bytes 56452
  714.0 98.4 %all-reduce.80.cloned.1.call-start = ((), (), s32[]{:S(2)}) async-start(), calls=%async_computation.4 | async-start | bytes 4718592 | tf_op jit(solution)/shard_map/psum | solution.py:181
  749.2 7.4 copy-start.4
  754.9 157.9 %all-reduce.82.cloned.1.call-start = ((), (), s32[]{:S(2)}) async-start(), calls=%async_computation.5 | async-start | bytes 4718592 | tf_op jit(solution)/shard_map/psum | solution.py:180
  756.7 55.8 %copy-start.32 = (bf16[96,384]{1,0:T(8,128)(2,1)S(1)}, bf16[96,384]{1,0:T(8,128)(2,1)}, u32[]{:S(2)}) copy-start(bf16[96,384]{1,0:T(8,128)(2,1)} %param.18) | copy-start | bytes 221188
  757.8 54.6 %copy-start.13 = (bf16[512,384]{1,0:T(8,128)(2,1)S(1)}, bf16[512,384]{1,0:T(8,128)(2,1)}, u32[]{:S(2)}) copy-start(bf16[512,384]{1,0:T(8,128)(2,1)} %copy-done.12) | copy-start | bytes 1179652
  757.8 55.0 %copy-start.34 = (f32[96]{0:T(128)S(1)}, f32[96]{0:T(128)}, u32[]{:S(2)}) copy-start(f32[96]{0:T(128)} %param.17) | copy-start | bytes 1156
  757.8 55.3 %copy-start.19 = (f32[8,8,8]{2,1,0:T(8,128)S(1)}, f32[8,8,8]{2,1,0:T(8,128)}, u32[]{:S(2)}) copy-start(f32[8,8,8]{2,1,0:T(8,128)} %copy-done.18) | copy-start | bytes 6148
  (23 other events, 106.7 us)
Sparse Core Ops, SparseCore 0:
  714.1 19.2 all-reduce.77
  755.0 57.3 all-reduce.79
  815.0 97.7 all-reduce.81
